TPU v7x, 32 devices: a whole 2x2x4 slice. The times are simulated.
32 devices in a mesh: row: 8 (over z, x), col: 4 (over y, core).
Axes of the slice: x: 2, y: 2, z: 4, core: 2. Of those that a mesh axis runs over, the one named last changes fastest.
Arguments:
- affinity: bfloat16 [32768, 8192], P('row', 'col'), may hold values from -250 to 250
- seed_values: int32 [16], replicated, may hold values from 0 to 1073741823
- sku_ids: int32 [8192], P('col'), may hold values from 0 to 8191, each once
Outputs:
- range_basis: float32 [16, 32768], P(None, ('row', 'col'))
- range_factor: float32 [16, 16], replicated
All inputs are finite; a program needn't handle non-finite values.
Results may differ from a plain program's by a relative error of at most 0.0046.
Values may be sent and summed in bfloat16 or wider, within the bound.
A program may use at most 64 MiB of HBM per device.

v0:
```python
import math
import jax
import jax.numpy as jnp
from jax import lax
from jax.sharding import PartitionSpec as P

ITERS = 2
mix_first = -2048144789
mix_second = -1028477387
golden = -1640531535
salt_value = 1540483477


def shifted(value, amount):
    return lax.shift_right_logical(value, jnp.full(value.shape, amount, jnp.int32))


def scramble(value):
    value = jnp.bitwise_xor(value, shifted(value, 16))
    value = value * jnp.int32(mix_first)
    value = jnp.bitwise_xor(value, shifted(value, 13))
    value = value * jnp.int32(mix_second)
    return jnp.bitwise_xor(value, shifted(value, 16))


def test_matrix(seed_values, sku_ids, total_columns):
    first = scramble(jnp.bitwise_xor(seed_values[:, None], sku_ids[None, :] * jnp.int32(golden)))
    second = scramble(jnp.bitwise_xor(first, jnp.int32(salt_value)))
    uniform_a = (shifted(first, 9) + 1).astype(jnp.float32) / 8388608.0
    uniform_b = (shifted(second, 9) + 1).astype(jnp.float32) / 8388608.0
    gauss = jnp.sqrt(-2.0 * jnp.log(uniform_a)) * jnp.cos(6.283185307179586 * uniform_b)
    return (gauss / math.sqrt(total_columns)).astype(jnp.bfloat16)


def lower_solve(lower, right):
    return lax.linalg.triangular_solve(lower, right, left_side=True, lower=True)


def body(affinity, seed_values, sku_ids):
    col_count = lax.axis_size("col")
    total_columns = sku_ids.shape[0] * col_count
    local_rows = affinity.shape[0]
    piece_rows = local_rows // col_count
    total_rows = local_rows * lax.axis_size("row")
    inv_root = 1.0 / math.sqrt(total_columns)

    def project(left):
        return lax.dot_general(
            left, affinity, (((1,), (1,)), ((), ())), preferred_element_type=jnp.float32
        )

    omega = test_matrix(seed_values, sku_ids, total_columns)
    partial_sketch = project(omega)
    for repeat in range(ITERS + 1):
        sketch = lax.psum(partial_sketch, "col")
        gram = lax.psum(
            jnp.dot(
                sketch,
                sketch.T,
                precision=lax.Precision.HIGHEST,
                preferred_element_type=jnp.float32,
            ),
            "row",
        )
        lower = jnp.linalg.cholesky(gram)
        ortho = lower_solve(lower, sketch)
        if repeat < ITERS:
            back_part = jnp.dot(
                ortho.astype(jnp.bfloat16), affinity, preferred_element_type=jnp.float32
            )
        else:
            start_row = lax.axis_index("col") * piece_rows
            ortho = lax.dynamic_slice_in_dim(ortho, start_row, piece_rows, 1)
        if repeat < ITERS:
            back = lax.psum(back_part, "row")
            partial_sketch = project(back.astype(jnp.bfloat16)) * inv_root
    scale = math.sqrt(total_rows)
    return (ortho * scale, lower.T / scale)


def solution(mesh):
    placed = (P("row", "col"), P(), P("col"))
    return jax.shard_map(
        body, mesh=mesh, in_specs=placed, out_specs=(P(None, ("row", "col")), P()), check_vma=False
    )
```

profile of v0, /device:TPU:0, one launch (start us, length us, event | category | flops | bytes accessed | tf_op | source)
XLA Modules:
  0.0 315.6 jit_solution(10747152659197352157)
XLA Ops:
  7.2 0.0 all-reduce.6.cloned.1.call-start
  7.2 0.7 broadcast_multiply_fusion
  7.9 11.5 %fusion.12 = f32[16,4096]{1,0:T(8,128)} fusion(bf16[4096,2048]{1,0:T(8,128)(2,1)} %param.6, s32[2048]{0:T(1024)S(1)} %broadcast_multiply_fusion, s32[16]{0:T(128)} %param.7), kind=kOutput, calls=%fused_computation.22 | convolution fusion | flops 269418496 | bytes 17047616 | tf_op jit(solution)/shard_map/dot_general | solution.py:48
  19.5 0.0 all-reduce.6.cloned.1.call-update
  19.5 0.0 all-reduce.8.cloned.1.call-start
  19.5 35.1 %all-reduce.6.cloned.1.call-done = f32[16,4096]{1,0:T(8,128)} async-done(((f32[16,4096]{1,0:T(8,128)}), f32[16,4096]{1,0:T(8,128)}) %all-reduce.6.cloned.1.call-update) | async-done | bytes 262160 | tf_op jit(solution)/shard_map/psum | solution.py:55
  54.6 1.5 fusion.54
  56.1 21.6 %psum.57 = f32[16,16]{0,1:T(8,128)S(1)} all-reduce(f32[16,16]{0,1:T(8,128)S(1)} %fusion.54), channel_id=1, replica_groups=mesh['row'=8,'col'=4] {'row'}, use_global_device_ids=true, to_apply=%region_1.0 | all-reduce | flops 256 | bytes 2048 | tf_op jit(solution)/shard_map/psum | solution.py:56
  77.7 0.1 copy.6
  77.8 1.5 cholesky.59
  79.3 0.6 compare_reduce_fusion.2
  79.9 0.6 fusion.29
  80.6 1.2 custom-call.7
  81.8 1.4 convolution_convert_fusion.1
  83.2 8.0 %fusion.55 = f32[16,2048]{1,0:T(8,128)S(1)} fusion(bf16[16,4096]{1,0:T(8,128)(2,1)S(1)} %convolution_convert_fusion.1, bf16[4096,2048]{1,0:T(8,128)(2,1)} %param.6), kind=kOutput, calls=%fused_computation.79 | convolution fusion | flops 268435456 | bytes 17039360 | tf_op jit(solution)/shard_map/dot_general | solution.py:68
  91.3 34.2 %all-reduce.11 = bf16[16,2048]{1,0:T(8,128)(2,1)S(1)} all-reduce(f32[16,2048]{1,0:T(8,128)S(1)} %fusion.55), channel_id=1, replica_groups=mesh['row'=8,'col'=4] {'row'}, use_global_device_ids=true, to_apply=%region_4.7 | all-reduce | flops 32768 | bytes 196608 | tf_op jit(solution)/shard_map/psum | solution.py:75
  125.5 10.9 %convolution_multiply_fusion.1 = f32[16,4096]{1,0:T(8,128)} fusion(bf16[4096,2048]{1,0:T(8,128)(2,1)} %param.6, bf16[16,2048]{1,0:T(8,128)(2,1)S(1)} %all-reduce.11), kind=kOutput, calls=%fused_computation.1 | convolution fusion | flops 268500992 | bytes 17104896 | tf_op jit(solution)/shard_map/dot_general | solution.py:48
  136.4 0.0 all-reduce.8.cloned.1.call-update
  136.4 0.0 all-reduce.10.cloned.1.call-start
  136.5 30.3 %all-reduce.8.cloned.1.call-done = f32[16,4096]{1,0:T(8,128)} async-done(((f32[16,4096]{1,0:T(8,128)}), f32[16,4096]{1,0:T(8,128)}) %all-reduce.8.cloned.1.call-update) | async-done | bytes 262160 | tf_op jit(solution)/shard_map/psum | solution.py:55
  166.8 1.5 fusion.56
  168.3 21.8 %psum.60 = f32[16,16]{0,1:T(8,128)S(1)} all-reduce(f32[16,16]{0,1:T(8,128)S(1)} %fusion.56), channel_id=1, replica_groups=mesh['row'=8,'col'=4] {'row'}, use_global_device_ids=true, to_apply=%region_6.9 | all-reduce | flops 256 | bytes 2048 | tf_op jit(solution)/shard_map/psum | solution.py:56
  190.1 0.1 copy.8
  190.2 1.5 cholesky.70
  191.6 0.6 compare_reduce_fusion.1
  192.3 0.6 fusion.30
  192.9 1.2 custom-call.8
  194.2 1.4 convolution_convert_fusion
  195.6 8.0 %fusion.57 = f32[16,2048]{1,0:T(8,128)S(1)} fusion(bf16[16,4096]{1,0:T(8,128)(2,1)S(1)} %convolution_convert_fusion, bf16[4096,2048]{1,0:T(8,128)(2,1)} %param.6), kind=kOutput, calls=%fused_computation.81 | convolution fusion | flops 268435456 | bytes 17039360 | tf_op jit(solution)/shard_map/dot_general | solution.py:68
  203.6 34.2 %all-reduce.12 = bf16[16,2048]{1,0:T(8,128)(2,1)S(1)} all-reduce(f32[16,2048]{1,0:T(8,128)S(1)} %fusion.57), channel_id=1, replica_groups=mesh['row'=8,'col'=4] {'row'}, use_global_device_ids=true, to_apply=%region_7.10 | all-reduce | flops 32768 | bytes 196608 | tf_op jit(solution)/shard_map/psum | solution.py:75
  237.8 10.9 %convolution_multiply_fusion = f32[16,4096]{1,0:T(8,128)} fusion(bf16[4096,2048]{1,0:T(8,128)(2,1)} %param.6, bf16[16,2048]{1,0:T(8,128)(2,1)S(1)} %all-reduce.12), kind=kOutput, calls=%fused_computation | convolution fusion | flops 268500992 | bytes 17104896 | tf_op jit(solution)/shard_map/dot_general | solution.py:48
  248.7 0.0 all-reduce.10.cloned.1.call-update
  248.8 30.4 %all-reduce.10.cloned.1.call-done = f32[16,4096]{1,0:T(8,128)} async-done(((f32[16,4096]{1,0:T(8,128)}), f32[16,4096]{1,0:T(8,128)}) %all-reduce.10.cloned.1.call-update) | async-done | bytes 262160 | tf_op jit(solution)/shard_map/psum | solution.py:55
  279.2 1.5 fusion.58
  280.6 21.6 %psum.63 = f32[16,16]{0,1:T(8,128)S(1)} all-reduce(f32[16,16]{0,1:T(8,128)S(1)} %fusion.58), channel_id=1, replica_groups=mesh['row'=8,'col'=4] {'row'}, use_global_device_ids=true, to_apply=%region_9.12 | all-reduce | flops 256 | bytes 2048 | tf_op jit(solution)/shard_map/psum | solution.py:56
  302.3 0.1 copy.10
  302.3 1.5 cholesky.81
  303.8 0.6 compare_reduce_fusion
  304.5 0.7 multiply_bitcast_fusion
  305.1 1.2 custom-call.9
  306.4 0.7 copy.11
  307.0 1.4 fusion.31
  308.4 0.6 dynamic-slice_multiply_fusion
  (6 shorter events, 0.1 us)
Async XLA Ops:
  7.2 47.5 %all-reduce.6.cloned.1.call-start = ((), (), s32[]{:S(2)}) async-start(), calls=%async_computation | async-start | bytes 524288 | tf_op jit(solution)/shard_map/psum | solution.py:55
  19.5 147.3 %all-reduce.8.cloned.1.call-start = ((), (), s32[]{:S(2)}) async-start(), calls=%async_computation.1 | async-start | bytes 524288 | tf_op jit(solution)/shard_map/psum | solution.py:55
  136.4 142.8 %all-reduce.10.cloned.1.call-start = ((), (), s32[]{:S(2)}) async-start(), calls=%async_computation.2 | async-start | bytes 524288 | tf_op jit(solution)/shard_map/psum | solution.py:55
Sparse Core Ops, SparseCore 0:
  19.6 34.9 all-reduce.5
  136.5 30.2 all-reduce.7
  248.9 30.2 all-reduce.9
where the time goes:
time: 316 us
  blocking collectives  133 us (42%)
  waiting for transfers between devices  95.9 us (30%)
  matrix products  58 us (18%)
  between operations  13.8 us (4%)
  other arithmetic  13.4 us (4%)
    psum x3, waiting for transfers between devices, body(): sketch = lax.psum(partial_sketch, 'col')  95.9 us
    psum x2, blocking collectives, body(): back = lax.psum(back_part, 'row')  68.4 us
    psum x3, blocking collectives, body(): lax.psum(jnp.dot(sketch, sketch.T, precision=lax.Precision.HIGHEST, prefe...  65 us
    dot_general x3, matrix products, project(): lax.dot_general(left, affinity, (((1,), (1,)), ((), ())), preferred_eleme...  33.4 us
    dot_general x2, matrix products, body(): jnp.dot(ortho.astype(jnp.bfloat16), affinity, preferred_element_type=jnp....  16.1 us
    another operation x9, other arithmetic, body(): lower = jnp.linalg.cholesky(gram)  6.39 us
  transfers between devices with their start and end apart: 3, of which 3 were waited for; matrix products, arithmetic and copies ran while one was open for 0% of the time, Pallas kernels for 0%

commit v1 on v0

--- a/solution.py
+++ b/solution.py
@@ -52,7 +52,9 @@
     omega = test_matrix(seed_values, sku_ids, total_columns)
     partial_sketch = project(omega)
     for repeat in range(ITERS + 1):
-        sketch = lax.psum(partial_sketch, "col")
+        sketch = partial_sketch
+        for hop in (1, 2):
+            sketch = sketch + lax.ppermute(sketch, "col", [(dev, dev ^ hop) for dev in range(4)])
         gram = lax.psum(
             jnp.dot(
                 sketch,

time: 316 us -> 227 us (0.72)
  waiting for transfers between devices: 95.9 us -> 24.5 us
  between operations: 13.8 us -> 0.75 us
  matrix products: 58 us -> 50 us
  starting transfers between devices: 0.12 us -> 6.63 us
    psum x3 -> x0, waiting for transfers between devices: 95.9 us -> none  [body(): sketch = lax.psum(partial_sketch, 'col')]
    ppermute x0 -> x6, waiting for transfers between devices: none -> 24.5 us  [body(): lax.ppermute(sketch, 'col', [(dev, dev ^ hop) for dev in range(4)])]
    ppermute x0 -> x6, starting transfers between devices: none -> 6.63 us  [body(): lax.ppermute(sketch, 'col', [(dev, dev ^ hop) for dev in range(4)])]
    psum x3, blocking collectives: 65 us -> 61.5 us  [body(): lax.psum(jnp.dot(sketch, sketch.T, precision=lax.Precision.HIGHEST, prefe...]
  transfers between devices with their start and end apart: 3 -> 6, of which waited for: 3 -> 6; matrix products, arithmetic and copies ran while one was open for 0% -> 0% of each run, Pallas kernels for 0% -> 0%
where the time goes in v1:
time: 227 us; the launch traced here: 226 us
  blocking collectives  130 us (57%)
  matrix products  50 us (22%)
  waiting for transfers between devices  24.5 us (11%)
  other arithmetic  13.6 us (6%)
  starting transfers between devices  6.63 us (3%)
    psum x2, blocking collectives, body(): back = lax.psum(back_part, 'row')  68.4 us
    psum x3, blocking collectives, body(): lax.psum(jnp.dot(sketch, sketch.T, precision=lax.Precision.HIGHEST, prefe...  61.5 us
    dot_general x3, matrix products, project(): lax.dot_general(left, affinity, (((1,), (1,)), ((), ())), preferred_eleme...  31.2 us
    ppermute x6, waiting for transfers between devices, body(): lax.ppermute(sketch, 'col', [(dev, dev ^ hop) for dev in range(4)])  24.5 us
    dot_general x2, matrix products, body(): jnp.dot(ortho.astype(jnp.bfloat16), affinity, preferred_element_type=jnp....  16.1 us
    ppermute x6, starting transfers between devices, body(): lax.ppermute(sketch, 'col', [(dev, dev ^ hop) for dev in range(4)])  6.63 us
    another operation x9, other arithmetic, body(): lower = jnp.linalg.cholesky(gram)  6.39 us
    another operation x5, other arithmetic, lower_solve(): return lax.linalg.triangular_solve(lower, right, left_side=True, lower=True)  4.98 us
  transfers between devices with their start and end apart: 6, of which 6 were waited for; matrix products, arithmetic and copies ran while one was open for 0% of the time, Pallas kernels for 0%

profile of v1, /device:TPU:0, one launch (start us, length us, event | category | flops | bytes accessed | tf_op | source)
XLA Modules:
  0.0 226.3 jit_solution(201377899414715962)
XLA Ops:
  0.6 0.7 broadcast_multiply_fusion
  1.3 10.8 %fusion.12 = f32[16,4096]{1,0:T(8,128)S(1)} fusion(bf16[4096,2048]{1,0:T(8,128)(2,1)} %param.6, s32[2048]{0:T(1024)S(1)} %broadcast_multiply_fusion, s32[16]{0:T(128)} %param.7), kind=kOutput, calls=%fused_computation.22 | convolution fusion | flops 269418496 | bytes 17047616 | tf_op jit(solution)/shard_map/dot_general | solution.py:48
  12.2 0.5 collective-permute-start
  12.7 1.2 collective-permute-done
  13.9 2.9 %collective-permute-start.1 = (f32[16,4096]{1,0:T(8,128)S(1)}, f32[16,4096]{1,0:T(8,128)S(1)}, u32[]{:S(2)}, u32[]{:S(2)}) collective-permute-start(f32[16,4096]{1,0:T(8,128)S(1)} %add.47), channel_id=1, source_target_pairs={{0,2},{1,3},{2,0},{3,1},{4,6},{5,7},{6,4},{7,5},{8,10},{9,11},{10,... | collective-permute-start | bytes 786440 | tf_op jit(solution)/shard_map/ppermute | solution.py:57
  16.8 6.6 %collective-permute-done.1 = f32[16,4096]{1,0:T(8,128)S(1)} collective-permute-done((f32[16,4096]{1,0:T(8,128)S(1)}, f32[16,4096]{1,0:T(8,128)S(1)}, u32[]{:S(2)}, u32[]{:S(2)}) %collective-permute-start.1) | collective-permute-done | bytes 262176 | tf_op jit(solution)/shard_map/ppermute | solution.py:57
  23.4 0.5 fusion.54
  23.9 22.1 %psum.35 = f32[16,16]{0,1:T(8,128)S(1)} all-reduce(f32[16,16]{0,1:T(8,128)S(1)} %fusion.54), channel_id=1, replica_groups=mesh['row'=8,'col'=4] {'row'}, use_global_device_ids=true, to_apply=%region_0.0 | all-reduce | flops 256 | bytes 2048 | tf_op jit(solution)/shard_map/psum | solution.py:58
  46.0 0.1 copy.6
  46.1 1.5 cholesky.59
  47.6 0.6 compare_reduce_fusion.2
  48.2 0.6 fusion.29
  48.9 1.2 custom-call.7
  50.1 0.4 convolution_convert_fusion.1
  50.6 8.0 %fusion.55 = f32[16,2048]{1,0:T(8,128)S(1)} fusion(bf16[16,4096]{1,0:T(8,128)(2,1)S(1)} %convolution_convert_fusion.1, bf16[4096,2048]{1,0:T(8,128)(2,1)} %param.6), kind=kOutput, calls=%fused_computation.79 | convolution fusion | flops 268435456 | bytes 17039360 | tf_op jit(solution)/shard_map/dot_general | solution.py:70
  58.6 34.2 %all-reduce.2 = bf16[16,2048]{1,0:T(8,128)(2,1)S(1)} all-reduce(f32[16,2048]{1,0:T(8,128)S(1)} %fusion.55), channel_id=1, replica_groups=mesh['row'=8,'col'=4] {'row'}, use_global_device_ids=true, to_apply=%region_3.6 | all-reduce | flops 32768 | bytes 196608 | tf_op jit(solution)/shard_map/psum | solution.py:77
  92.8 10.2 %convolution_multiply_fusion.1 = f32[16,4096]{1,0:T(8,128)S(1)} fusion(bf16[4096,2048]{1,0:T(8,128)(2,1)} %param.6, bf16[16,2048]{1,0:T(8,128)(2,1)S(1)} %all-reduce.2), kind=kOutput, calls=%fused_computation.1 | convolution fusion | flops 268500992 | bytes 17104896 | tf_op jit(solution)/shard_map/dot_general | solution.py:48
  103.0 0.0 collective-permute-start.2
  103.0 1.5 collective-permute-done.2
  104.6 1.6 collective-permute-start.3
  106.2 6.8 %collective-permute-done.3 = f32[16,4096]{1,0:T(8,128)S(1)} collective-permute-done((f32[16,4096]{1,0:T(8,128)S(1)}, f32[16,4096]{1,0:T(8,128)S(1)}, u32[]{:S(2)}, u32[]{:S(2)}) %collective-permute-start.3) | collective-permute-done | bytes 262176 | tf_op jit(solution)/shard_map/ppermute | solution.py:57
  113.0 0.5 fusion.56
  113.5 19.8 %psum.37 = f32[16,16]{0,1:T(8,128)S(1)} all-reduce(f32[16,16]{0,1:T(8,128)S(1)} %fusion.56), channel_id=1, replica_groups=mesh['row'=8,'col'=4] {'row'}, use_global_device_ids=true, to_apply=%region_4.7 | all-reduce | flops 256 | bytes 2048 | tf_op jit(solution)/shard_map/psum | solution.py:58
  133.3 0.1 copy.8
  133.4 1.5 cholesky.70
  134.9 0.6 compare_reduce_fusion.1
  135.5 0.6 fusion.30
  136.2 1.2 custom-call.8
  137.4 0.4 convolution_convert_fusion
  137.9 8.0 %fusion.57 = f32[16,2048]{1,0:T(8,128)S(1)} fusion(bf16[16,4096]{1,0:T(8,128)(2,1)S(1)} %convolution_convert_fusion, bf16[4096,2048]{1,0:T(8,128)(2,1)} %param.6), kind=kOutput, calls=%fused_computation.81 | convolution fusion | flops 268435456 | bytes 17039360 | tf_op jit(solution)/shard_map/dot_general | solution.py:70
  145.9 34.3 %all-reduce.3 = bf16[16,2048]{1,0:T(8,128)(2,1)S(1)} all-reduce(f32[16,2048]{1,0:T(8,128)S(1)} %fusion.57), channel_id=1, replica_groups=mesh['row'=8,'col'=4] {'row'}, use_global_device_ids=true, to_apply=%region_5.8 | all-reduce | flops 32768 | bytes 196608 | tf_op jit(solution)/shard_map/psum | solution.py:77
  180.2 10.2 %convolution_multiply_fusion = f32[16,4096]{1,0:T(8,128)S(1)} fusion(bf16[4096,2048]{1,0:T(8,128)(2,1)} %param.6, bf16[16,2048]{1,0:T(8,128)(2,1)S(1)} %all-reduce.3), kind=kOutput, calls=%fused_computation | convolution fusion | flops 268500992 | bytes 17104896 | tf_op jit(solution)/shard_map/dot_general | solution.py:48
  190.4 0.0 collective-permute-start.4
  190.4 1.5 collective-permute-done.4
  191.9 1.6 collective-permute-start.5
  193.5 6.8 %collective-permute-done.5 = f32[16,4096]{1,0:T(8,128)S(1)} collective-permute-done((f32[16,4096]{1,0:T(8,128)S(1)}, f32[16,4096]{1,0:T(8,128)S(1)}, u32[]{:S(2)}, u32[]{:S(2)}) %collective-permute-start.5) | collective-permute-done | bytes 262176 | tf_op jit(solution)/shard_map/ppermute | solution.py:57
  200.4 0.5 fusion.58
  200.9 19.6 %psum.39 = f32[16,16]{0,1:T(8,128)S(1)} all-reduce(f32[16,16]{0,1:T(8,128)S(1)} %fusion.58), channel_id=1, replica_groups=mesh['row'=8,'col'=4] {'row'}, use_global_device_ids=true, to_apply=%region_6.9 | all-reduce | flops 256 | bytes 2048 | tf_op jit(solution)/shard_map/psum | solution.py:58
  220.4 0.1 copy.10
  220.5 1.5 cholesky.81
  222.0 0.6 compare_reduce_fusion
  222.6 0.7 multiply_bitcast_fusion
  223.3 1.2 custom-call.9
  224.5 0.4 fusion.31
  225.0 0.7 copy.11
  225.6 0.6 dynamic-slice_multiply_fusion
  (12 shorter events, 0.3 us)
Async XLA Ops:
  12.2 1.7 collective-permute-start
  13.9 9.5 %collective-permute-start.1 = (f32[16,4096]{1,0:T(8,128)S(1)}, f32[16,4096]{1,0:T(8,128)S(1)}, u32[]{:S(2)}, u32[]{:S(2)}) collective-permute-start(f32[16,4096]{1,0:T(8,128)S(1)} %add.47), channel_id=1, source_target_pairs={{0,2},{1,3},{2,0},{3,1},{4,6},{5,7},{6,4},{7,5},{8,10},{9,11},{10,... | collective-permute-start | bytes 786440 | tf_op jit(solution)/shard_map/ppermute | solution.py:57
  103.0 1.6 collective-permute-start.2
  104.6 8.4 %collective-permute-start.3 = (f32[16,4096]{1,0:T(8,128)S(1)}, f32[16,4096]{1,0:T(8,128)S(1)}, u32[]{:S(2)}, u32[]{:S(2)}) collective-permute-start(f32[16,4096]{1,0:T(8,128)S(1)} %add.49), channel_id=1, source_target_pairs={{0,2},{1,3},{2,0},{3,1},{4,6},{5,7},{6,4},{7,5},{8,10},{9,11},{10,... | collective-permute-start | bytes 786440 | tf_op jit(solution)/shard_map/ppermute | solution.py:57
  190.4 1.6 collective-permute-start.4
  191.9 8.4 %collective-permute-start.5 = (f32[16,4096]{1,0:T(8,128)S(1)}, f32[16,4096]{1,0:T(8,128)S(1)}, u32[]{:S(2)}, u32[]{:S(2)}) collective-permute-start(f32[16,4096]{1,0:T(8,128)S(1)} %add.51), channel_id=1, source_target_pairs={{0,2},{1,3},{2,0},{3,1},{4,6},{5,7},{6,4},{7,5},{8,10},{9,11},{10,... | collective-permute-start | bytes 786440 | tf_op jit(solution)/shard_map/ppermute | solution.py:57
